TPU v7x, 128 devices: a whole 4x4x4 slice. The times are simulated.
128 devices in a mesh: row: 8 (over x, y_lo), col: 8 (over z, core), band: 2 (over y_hi).
Axes of the slice: x: 4, y: 4 (y_hi: 2, y_lo: 2; y = y_hi * 2 + y_lo), z: 4, core: 2. Of those that a mesh axis runs over, the one named last changes fastest.
Arguments:
- freq_index: int32 [2], replicated, may hold values from 0 to 32
- band_energy: float32 [16], replicated, may hold values from -4 to 4
- pole_amp: float32 [8192, 8192], P('row', 'col'), may hold values from -6 to 6
- pole_freq: float32 [8192, 8192], P('row', 'col'), may hold values from 0.5 to 4
- left_pieces: bfloat16 [16, 256, 8192], P(('col', 'band'), None, 'row'), may hold values from -0.032958984 to 0.032958984
- right_pieces: bfloat16 [16, 256, 8192], P(('row', 'band'), None, 'col'), may hold values from -0.032958984 to 0.032958984
Outputs:
- sigma: float32 [2, 256, 256], P(None, ('row', 'col', 'band'))
All inputs are finite; a program needn't handle non-finite values.
Results may differ from a plain program's by a relative error of at most 0.0055.
Values may be sent and summed in bfloat16 or wider, within the bound.
A program may use at most 128 MiB of HBM per device.

v0:
```python
import jax
import jax.numpy as jnp
from jax import lax
from jax.sharding import Mesh
from jax.sharding import PartitionSpec as P

ROW = ("row_0", "row_1")
ROW_COL_BAND = ("row_0", "row_1", "col", "band")
ROW_BAND = ("row_0", "row_1", "band")


def whole_of(array, axes, dim):
    for axis in reversed(axes):
        array = lax.all_gather(array, axis, axis=dim, tiled=True)
    return array


def body(freq_index, band_energy, pole_amp, pole_freq, left_pieces, right_pieces):
    bpiece = left_pieces.shape[0]
    nstate = left_pieces.shape[1]
    nfreq = freq_index.shape[0]
    nband = lax.axis_size("band")
    group = lax.axis_index("band")
    freq = -4.0 + 0.25 * freq_index.astype(jnp.float32)
    right_all = whole_of(right_pieces, ROW, 0)

    def energy_at(position):
        overall = (position // bpiece * nband + group) * bpiece + position % bpiece
        return lax.dynamic_index_in_dim(band_energy, overall, 0, False)

    def add_band(total, left_band, position):
        right_band = lax.dynamic_index_in_dim(right_all, position, 0, False)
        energy = energy_at(position)
        results = []
        for w in range(nfreq):
            distance = freq[w] - energy - pole_freq
            screened = (pole_amp * distance / (distance * distance + 0.25)).astype(jnp.bfloat16)
            partial_value = jnp.dot(left_band, screened, preferred_element_type=jnp.float32).astype(
                jnp.bfloat16
            )
            results.append(
                lax.dot_general(
                    partial_value,
                    right_band,
                    (((1,), (1,)), ((), ())),
                    preferred_element_type=jnp.float32,
                )
            )
        return total + jnp.stack(results)

    start = jnp.zeros((nfreq, nstate, nstate), jnp.float32)
    left_all = lax.all_gather(left_pieces, "col", axis=0, tiled=True)

    def step(index, carry):
        left_band = lax.dynamic_index_in_dim(left_all, index, 0, False)
        return add_band(carry, left_band, index)

    total = lax.fori_loop(0, left_all.shape[0], step, start)
    summed = lax.psum(total, ROW_COL_BAND)
    owned = nstate // lax.axis_size(ROW_COL_BAND)
    sigma = lax.dynamic_slice_in_dim(summed, lax.axis_index(ROW_COL_BAND) * owned, owned, 1)
    return sigma


def solution(mesh):
    split = Mesh(
        mesh.devices.reshape(4, 2, mesh.shape["col"], mesh.shape["band"]),
        ("row_0", "row_1", "col", "band"),
    )
    in_specs = (
        P(),
        P(),
        P(ROW, "col"),
        P(ROW, "col"),
        P(("col", "band"), None, ROW),
        P(ROW_BAND, None, "col"),
    )
    out_specs = P(None, ROW_COL_BAND, None)
    return jax.shard_map(body, mesh=split, in_specs=in_specs, out_specs=out_specs, check_vma=False)
```

profile of v0, /device:TPU:1, one launch (start us, length us, event | category | flops | bytes accessed | tf_op | source)
XLA Modules:
  0.0 393.0 jit_solution(11050577234584993853)
XLA Ops:
  6.5 0.7 all-gather.6.cloned.1.call-update
  7.3 0.7 all-gather.4.cloned.1.call-update
  8.1 27.8 %all-gather.6.cloned.1.call-done = bf16[2,256,1024]{2,1,0:T(8,128)(2,1)} async-done(((bf16[1,256,1024]{2,1,0:T(8,128)(2,1)}), bf16[2,256,1024]{2,1,0:T(8,128)(2,1)}) %all-gather.6.cloned.1.call-update) | async-done | bytes 1048592 | tf_op jit(solution)/shard_map/all_gather | solution.py:14
  35.9 0.7 multiply_add_fusion
  36.6 34.8 %all-gather.4.cloned.1.call-done = bf16[8,256,1024]{2,1,0:T(8,128)(2,1)} async-done(((bf16[1,256,1024]{2,1,0:T(8,128)(2,1)}), bf16[8,256,1024]{2,1,0:T(8,128)(2,1)}) %all-gather.4.cloned.1.call-update) | async-done | bytes 4194320 | tf_op jit(solution)/shard_map/all_gather | solution.py:52
  71.4 49.1 %all-gather.8.cloned.1.call-done = bf16[8,256,1024]{2,1,0:T(8,128)(2,1)} async-done(((bf16[2,256,1024]{2,1,0:T(8,128)(2,1)}), bf16[8,256,1024]{2,1,0:T(8,128)(2,1)}) %all-gather.8.cloned.1.call-update) | async-done | bytes 4194320 | tf_op jit(solution)/shard_map/all_gather | solution.py:14
  120.5 116.6 %while.17 = (s32[]{:T(128)}, f32[2,256,256]{2,1,0:T(8,128)S(1)}, bf16[8,256,1024]{2,1,0:T(8,128)(2,1)}, f32[2]{0:T(128)S(1)}, s32[]{:T(128)}, /*index=5*/f32[16]...) while((s32[]{:T(128)}, f32[2,256,256]{2,1,0:T(8,128)S(1)}, ...), condition=%wide.region_1.2_spmd.clone, body=%wide.region_0.1_spmd.clone.sunk | while | flops 1355677696 | bytes 20974844 | solution.py:58
  120.5 1.2 dynamic_slice.70
  121.7 0.6 fusion.34
  124.7 5.1 %convolution_bitcast_fusion.4 = f32[1,256,256]{2,1,0:T(8,128)S(1)} fusion(f32[1024,1024]{1,0:T(8,128)} %get-tuple-element.398, f32[1024,1024]{1,0:T(8,128)} %get-tuple-element.397, f32[]{:T(128)} %bitcast.32, bf16[8,256,1024]{2,1,0:T(8,128)(2,1)} %get-tuple-element.399, s32[]{:T(128)S(6)} %copy.9, bf16[8,256,1024]{2,1,0:T(8,128)(2,1)} %get-tuple-element.393), kind=kOutput, calls=%fused_computation.6.clone.1 | convolution fusion | flops 677642240 | bytes 9700864 | tf_op jit(solution)/shard_map/while/body/eval_jaxpr/dot_general | solution.py:42
  129.8 5.1 %convolution_bitcast_fusion.5 = f32[1,256,256]{2,1,0:T(8,128)S(1)} fusion(f32[1024,1024]{1,0:T(8,128)} %get-tuple-element.398, f32[1024,1024]{1,0:T(8,128)} %get-tuple-element.397, f32[]{:T(128)} %bitcast.33, bf16[8,256,1024]{2,1,0:T(8,128)(2,1)} %get-tuple-element.399, s32[]{:T(128)S(6)} %copy.9, bf16[8,256,1024]{2,1,0:T(8,128)(2,1)} %get-tuple-element.393), kind=kOutput, calls=%fused_computation.7.clone.1 | convolution fusion | flops 677642240 | bytes 9700864 | tf_op jit(solution)/shard_map/while/body/eval_jaxpr/dot_general | solution.py:42
  134.9 0.1 maximum_add_fusion.2
  135.1 1.2 dynamic_slice.70
  136.3 0.6 fusion.34
  139.3 5.1 %convolution_bitcast_fusion.4 = f32[1,256,256]{2,1,0:T(8,128)S(1)} fusion(f32[1024,1024]{1,0:T(8,128)} %get-tuple-element.398, f32[1024,1024]{1,0:T(8,128)} %get-tuple-element.397, f32[]{:T(128)} %bitcast.32, bf16[8,256,1024]{2,1,0:T(8,128)(2,1)} %get-tuple-element.399, s32[]{:T(128)S(6)} %copy.9, bf16[8,256,1024]{2,1,0:T(8,128)(2,1)} %get-tuple-element.393), kind=kOutput, calls=%fused_computation.6.clone.1 | convolution fusion | flops 677642240 | bytes 9700864 | tf_op jit(solution)/shard_map/while/body/eval_jaxpr/dot_general | solution.py:42
  144.4 5.1 %convolution_bitcast_fusion.5 = f32[1,256,256]{2,1,0:T(8,128)S(1)} fusion(f32[1024,1024]{1,0:T(8,128)} %get-tuple-element.398, f32[1024,1024]{1,0:T(8,128)} %get-tuple-element.397, f32[]{:T(128)} %bitcast.33, bf16[8,256,1024]{2,1,0:T(8,128)(2,1)} %get-tuple-element.399, s32[]{:T(128)S(6)} %copy.9, bf16[8,256,1024]{2,1,0:T(8,128)(2,1)} %get-tuple-element.393), kind=kOutput, calls=%fused_computation.7.clone.1 | convolution fusion | flops 677642240 | bytes 9700864 | tf_op jit(solution)/shard_map/while/body/eval_jaxpr/dot_general | solution.py:42
  149.4 0.1 maximum_add_fusion.2
  149.6 1.2 dynamic_slice.70
  150.9 0.6 fusion.34
  153.9 5.1 %convolution_bitcast_fusion.4 = f32[1,256,256]{2,1,0:T(8,128)S(1)} fusion(f32[1024,1024]{1,0:T(8,128)} %get-tuple-element.398, f32[1024,1024]{1,0:T(8,128)} %get-tuple-element.397, f32[]{:T(128)} %bitcast.32, bf16[8,256,1024]{2,1,0:T(8,128)(2,1)} %get-tuple-element.399, s32[]{:T(128)S(6)} %copy.9, bf16[8,256,1024]{2,1,0:T(8,128)(2,1)} %get-tuple-element.393), kind=kOutput, calls=%fused_computation.6.clone.1 | convolution fusion | flops 677642240 | bytes 9700864 | tf_op jit(solution)/shard_map/while/body/eval_jaxpr/dot_general | solution.py:42
  159.0 5.1 %convolution_bitcast_fusion.5 = f32[1,256,256]{2,1,0:T(8,128)S(1)} fusion(f32[1024,1024]{1,0:T(8,128)} %get-tuple-element.398, f32[1024,1024]{1,0:T(8,128)} %get-tuple-element.397, f32[]{:T(128)} %bitcast.33, bf16[8,256,1024]{2,1,0:T(8,128)(2,1)} %get-tuple-element.399, s32[]{:T(128)S(6)} %copy.9, bf16[8,256,1024]{2,1,0:T(8,128)(2,1)} %get-tuple-element.393), kind=kOutput, calls=%fused_computation.7.clone.1 | convolution fusion | flops 677642240 | bytes 9700864 | tf_op jit(solution)/shard_map/while/body/eval_jaxpr/dot_general | solution.py:42
  164.0 0.1 maximum_add_fusion.2
  164.2 1.2 dynamic_slice.70
  165.5 0.6 fusion.34
  168.5 5.1 %convolution_bitcast_fusion.4 = f32[1,256,256]{2,1,0:T(8,128)S(1)} fusion(f32[1024,1024]{1,0:T(8,128)} %get-tuple-element.398, f32[1024,1024]{1,0:T(8,128)} %get-tuple-element.397, f32[]{:T(128)} %bitcast.32, bf16[8,256,1024]{2,1,0:T(8,128)(2,1)} %get-tuple-element.399, s32[]{:T(128)S(6)} %copy.9, bf16[8,256,1024]{2,1,0:T(8,128)(2,1)} %get-tuple-element.393), kind=kOutput, calls=%fused_computation.6.clone.1 | convolution fusion | flops 677642240 | bytes 9700864 | tf_op jit(solution)/shard_map/while/body/eval_jaxpr/dot_general | solution.py:42
  173.5 5.1 %convolution_bitcast_fusion.5 = f32[1,256,256]{2,1,0:T(8,128)S(1)} fusion(f32[1024,1024]{1,0:T(8,128)} %get-tuple-element.398, f32[1024,1024]{1,0:T(8,128)} %get-tuple-element.397, f32[]{:T(128)} %bitcast.33, bf16[8,256,1024]{2,1,0:T(8,128)(2,1)} %get-tuple-element.399, s32[]{:T(128)S(6)} %copy.9, bf16[8,256,1024]{2,1,0:T(8,128)(2,1)} %get-tuple-element.393), kind=kOutput, calls=%fused_computation.7.clone.1 | convolution fusion | flops 677642240 | bytes 9700864 | tf_op jit(solution)/shard_map/while/body/eval_jaxpr/dot_general | solution.py:42
  178.6 0.1 maximum_add_fusion.2
  178.8 1.2 dynamic_slice.70
  180.0 0.6 fusion.34
  183.0 5.1 %convolution_bitcast_fusion.4 = f32[1,256,256]{2,1,0:T(8,128)S(1)} fusion(f32[1024,1024]{1,0:T(8,128)} %get-tuple-element.398, f32[1024,1024]{1,0:T(8,128)} %get-tuple-element.397, f32[]{:T(128)} %bitcast.32, bf16[8,256,1024]{2,1,0:T(8,128)(2,1)} %get-tuple-element.399, s32[]{:T(128)S(6)} %copy.9, bf16[8,256,1024]{2,1,0:T(8,128)(2,1)} %get-tuple-element.393), kind=kOutput, calls=%fused_computation.6.clone.1 | convolution fusion | flops 677642240 | bytes 9700864 | tf_op jit(solution)/shard_map/while/body/eval_jaxpr/dot_general | solution.py:42
  188.1 5.1 %convolution_bitcast_fusion.5 = f32[1,256,256]{2,1,0:T(8,128)S(1)} fusion(f32[1024,1024]{1,0:T(8,128)} %get-tuple-element.398, f32[1024,1024]{1,0:T(8,128)} %get-tuple-element.397, f32[]{:T(128)} %bitcast.33, bf16[8,256,1024]{2,1,0:T(8,128)(2,1)} %get-tuple-element.399, s32[]{:T(128)S(6)} %copy.9, bf16[8,256,1024]{2,1,0:T(8,128)(2,1)} %get-tuple-element.393), kind=kOutput, calls=%fused_computation.7.clone.1 | convolution fusion | flops 677642240 | bytes 9700864 | tf_op jit(solution)/shard_map/while/body/eval_jaxpr/dot_general | solution.py:42
  193.2 0.1 maximum_add_fusion.2
  193.4 1.2 dynamic_slice.70
  194.6 0.6 fusion.34
  197.6 5.1 %convolution_bitcast_fusion.4 = f32[1,256,256]{2,1,0:T(8,128)S(1)} fusion(f32[1024,1024]{1,0:T(8,128)} %get-tuple-element.398, f32[1024,1024]{1,0:T(8,128)} %get-tuple-element.397, f32[]{:T(128)} %bitcast.32, bf16[8,256,1024]{2,1,0:T(8,128)(2,1)} %get-tuple-element.399, s32[]{:T(128)S(6)} %copy.9, bf16[8,256,1024]{2,1,0:T(8,128)(2,1)} %get-tuple-element.393), kind=kOutput, calls=%fused_computation.6.clone.1 | convolution fusion | flops 677642240 | bytes 9700864 | tf_op jit(solution)/shard_map/while/body/eval_jaxpr/dot_general | solution.py:42
  202.7 5.1 %convolution_bitcast_fusion.5 = f32[1,256,256]{2,1,0:T(8,128)S(1)} fusion(f32[1024,1024]{1,0:T(8,128)} %get-tuple-element.398, f32[1024,1024]{1,0:T(8,128)} %get-tuple-element.397, f32[]{:T(128)} %bitcast.33, bf16[8,256,1024]{2,1,0:T(8,128)(2,1)} %get-tuple-element.399, s32[]{:T(128)S(6)} %copy.9, bf16[8,256,1024]{2,1,0:T(8,128)(2,1)} %get-tuple-element.393), kind=kOutput, calls=%fused_computation.7.clone.1 | convolution fusion | flops 677642240 | bytes 9700864 | tf_op jit(solution)/shard_map/while/body/eval_jaxpr/dot_general | solution.py:42
  207.8 0.1 maximum_add_fusion.2
  208.0 1.2 dynamic_slice.70
  209.2 0.6 fusion.34
  212.2 5.1 %convolution_bitcast_fusion.4 = f32[1,256,256]{2,1,0:T(8,128)S(1)} fusion(f32[1024,1024]{1,0:T(8,128)} %get-tuple-element.398, f32[1024,1024]{1,0:T(8,128)} %get-tuple-element.397, f32[]{:T(128)} %bitcast.32, bf16[8,256,1024]{2,1,0:T(8,128)(2,1)} %get-tuple-element.399, s32[]{:T(128)S(6)} %copy.9, bf16[8,256,1024]{2,1,0:T(8,128)(2,1)} %get-tuple-element.393), kind=kOutput, calls=%fused_computation.6.clone.1 | convolution fusion | flops 677642240 | bytes 9700864 | tf_op jit(solution)/shard_map/while/body/eval_jaxpr/dot_general | solution.py:42
  217.3 5.1 %convolution_bitcast_fusion.5 = f32[1,256,256]{2,1,0:T(8,128)S(1)} fusion(f32[1024,1024]{1,0:T(8,128)} %get-tuple-element.398, f32[1024,1024]{1,0:T(8,128)} %get-tuple-element.397, f32[]{:T(128)} %bitcast.33, bf16[8,256,1024]{2,1,0:T(8,128)(2,1)} %get-tuple-element.399, s32[]{:T(128)S(6)} %copy.9, bf16[8,256,1024]{2,1,0:T(8,128)(2,1)} %get-tuple-element.393), kind=kOutput, calls=%fused_computation.7.clone.1 | convolution fusion | flops 677642240 | bytes 9700864 | tf_op jit(solution)/shard_map/while/body/eval_jaxpr/dot_general | solution.py:42
  222.5 1.2 dynamic_slice.70
  223.8 0.6 fusion.34
  226.8 5.1 %convolution_bitcast_fusion.4 = f32[1,256,256]{2,1,0:T(8,128)S(1)} fusion(f32[1024,1024]{1,0:T(8,128)} %get-tuple-element.398, f32[1024,1024]{1,0:T(8,128)} %get-tuple-element.397, f32[]{:T(128)} %bitcast.32, bf16[8,256,1024]{2,1,0:T(8,128)(2,1)} %get-tuple-element.399, s32[]{:T(128)S(6)} %copy.9, bf16[8,256,1024]{2,1,0:T(8,128)(2,1)} %get-tuple-element.393), kind=kOutput, calls=%fused_computation.6.clone.1 | convolution fusion | flops 677642240 | bytes 9700864 | tf_op jit(solution)/shard_map/while/body/eval_jaxpr/dot_general | solution.py:42
  231.9 5.1 %convolution_bitcast_fusion.5 = f32[1,256,256]{2,1,0:T(8,128)S(1)} fusion(f32[1024,1024]{1,0:T(8,128)} %get-tuple-element.398, f32[1024,1024]{1,0:T(8,128)} %get-tuple-element.397, f32[]{:T(128)} %bitcast.33, bf16[8,256,1024]{2,1,0:T(8,128)(2,1)} %get-tuple-element.399, s32[]{:T(128)S(6)} %copy.9, bf16[8,256,1024]{2,1,0:T(8,128)(2,1)} %get-tuple-element.393), kind=kOutput, calls=%fused_computation.7.clone.1 | convolution fusion | flops 677642240 | bytes 9700864 | tf_op jit(solution)/shard_map/while/body/eval_jaxpr/dot_general | solution.py:42
  237.1 0.8 copy-done
  237.9 147.2 %all-reduce.2.cloned.1.call-done = f32[2,256,256]{2,1,0:T(8,128)} async-done(((f32[2,256,256]{2,1,0:T(8,128)}), f32[2,256,256]{2,1,0:T(8,128)}) %all-reduce.2.cloned.1.call-update) | async-done | bytes 524304 | tf_op jit(solution)/shard_map/psum | solution.py:59
  385.1 1.3 constant_dynamic-slice_fusion
  (10 shorter events, 0.4 us)
Async XLA Ops:
  6.5 29.3 %all-gather.6.cloned.1.call-start = ((), (), s32[]{:S(2)}) async-start(), calls=%async_computation.1 | async-start | bytes 1572864 | tf_op jit(solution)/shard_map/all_gather | solution.py:14
  7.3 64.2 %all-gather.4.cloned.1.call-start = ((), (), s32[]{:S(2)}) async-start(), calls=%async_computation | async-start | bytes 4718592 | tf_op jit(solution)/shard_map/all_gather | solution.py:52
  8.0 112.5 %all-gather.8.cloned.1.call-start = ((), (), s32[]{:S(2)}) async-start(), calls=%async_computation.2 | async-start | bytes 5242880 | tf_op jit(solution)/shard_map/all_gather | solution.py:14
  35.9 349.2 %all-reduce.2.cloned.1.call-start = ((), (), s32[]{:S(2)}) async-start(), calls=%async_computation.3 | async-start | bytes 1048576 | tf_op jit(solution)/shard_map/psum | solution.py:59
  237.1 0.8 copy-start
Sparse Core Ops, SparseCore 0:
  9.0 26.8 all-gather.5
  37.6 33.7 all-gather.3
  73.1 47.3 all-gather.7
  238.0 147.0 all-reduce.1
where the time goes:
time: 393 us
  waiting for transfers between devices  260 us (66%)
  matrix products  81.2 us (21%)
  loops' own time  19.2 us (5%)
  local copies, waits for them, and re-layouts  17.1 us (4%)
  between operations  13.2 us (3%)
    psum x1, waiting for transfers between devices, body(): summed = lax.psum(total, ROW_COL_BAND)  147 us
    dot_general x16, matrix products, add_band(): lax.dot_general(partial_value, right_band, (((1,), (1,)), ((), ())), pref...  81.2 us
    all_gather x2, waiting for transfers between devices, whole_of(): array = lax.all_gather(array, axis, axis=dim, tiled=True)  76.9 us
    all_gather x1, waiting for transfers between devices, body(): left_all = lax.all_gather(left_pieces, 'col', axis=0, tiled=True)  34.8 us
    another operation x1, loops' own time, body(): total = lax.fori_loop(0, left_all.shape[0], step, start)  19.2 us
    dynamic_slice x8, local copies, waits for them, and re-layouts, energy_at(): return lax.dynamic_index_in_dim(band_energy, overall, 0, False)  9.87 us
  transfers between devices with their start and end apart: 4, of which 4 were waited for; matrix products, arithmetic and copies ran while one was open for 0% of the time, Pallas kernels for 0%

commit v1 on v0

v1 whole, which is shorter than its diff:
```python
import jax
import jax.numpy as jnp
from jax import lax
from jax.experimental import pallas as pl
from jax.experimental.pallas import tpu as pltpu
from jax.sharding import PartitionSpec as P

MESH = pl.DeviceIdType.MESH
F32 = jnp.float32
BF16 = jnp.bfloat16

NST = 256
TILE = 1024
HALF = NST // 2
CHUNK = 512
NCHUNK = TILE // CHUNK
LANES = 128


def kernel(freq_index, band_energy, pole_freq, pole_amp, left, right, out,
           pf, pa, lbuf, rbuf, ubuf, sig, tiles, in_a, vx, in_x, vy, in_y, vz, in_z,
           load_sem, own_sem, lsend, lrecv, rsend, rrecv, ssend, srecv):
    row, col, yhi = lax.axis_index("row"), lax.axis_index("col"), lax.axis_index("band")
    x, ylo, z, core = row // 2, row % 2, col // 2, col % 2
    y = yhi * 2 + ylo

    def device(dx=0, dy=0, dz=0, dc=0, flip=0):
        yy = (y + dy) % 4
        return {
            "row": ((x + dx) % 4) * 2 + (yy % 2 + flip) % 2,
            "col": ((z + dz) % 4) * 2 + (core + dc) % 2,
            "band": yy // 2,
        }

    def pole_copies(c):
        cs = pl.ds(pl.multiple_of(c * CHUNK, CHUNK), CHUNK)
        return (
            pltpu.make_async_copy(pole_freq.at[:, cs], pf.at[:, cs], load_sem.at[c]),
            pltpu.make_async_copy(pole_amp.at[:, cs], pa.at[:, cs], load_sem.at[NCHUNK + c]),
        )

    own_l = pltpu.make_async_copy(left.at[0], lbuf.at[0], own_sem.at[0])
    own_r = pltpu.make_async_copy(right.at[0], rbuf.at[0], own_sem.at[1])
    own_l.start()
    for c in range(NCHUNK):
        for copy in pole_copies(c):
            copy.start()
    own_r.start()

    barrier = pltpu.get_barrier_semaphore()
    peers = [device(dc=1)]
    for k in (1, 2, 3):
        peers += [device(dx=k), device(dy=k), device(dz=k)]
    for peer in peers:
        pl.semaphore_signal(barrier, inc=1, device_id=peer, device_id_type=MESH)
    pl.semaphore_wait(barrier, len(peers))

    started = []

    def send(src, dst, send_sem, recv_sem, to):
        copy = pltpu.make_async_remote_copy(
            src_ref=src, dst_ref=dst, send_sem=send_sem, recv_sem=recv_sem,
            device_id=to, device_id_type=MESH,
        )
        copy.start()
        started.append(copy)
        return copy

    lo, hi = pl.ds(0, HALF), pl.ds(HALF, HALF)

    l_c1 = send(left.at[0], lbuf.at[1], lsend.at[0], lrecv.at[0], device(dc=1))
    r_y1 = send(right.at[0], rbuf.at[1], rsend.at[0], rrecv.at[0], device(flip=1))
    l_zm = send(left.at[0], lbuf.at[6], lsend.at[1], lrecv.at[1], device(dz=1))
    l_zp = send(left.at[0], lbuf.at[2], lsend.at[2], lrecv.at[2], device(dz=3))
    r_xm = send(right.at[0], rbuf.at[6], rsend.at[1], rrecv.at[1], device(dx=1))
    r_xp = send(right.at[0], rbuf.at[2], rsend.at[2], rrecv.at[2], device(dx=3))

    def scalars(slot):
        zs, cs = (z + slot // 2) % 4, (core + slot) % 2
        energy = band_energy[(zs * 2 + cs) * 2 + yhi]
        return [-4.0 + 0.25 * freq_index[w].astype(F32) - energy for w in range(2)]

    def first(slot, c):
        cs = pl.ds(pl.multiple_of(c * CHUNK, CHUNK), CHUNK)
        shifts = scalars(slot)
        for w in range(2):
            d = shifts[w] - pf[:, cs]
            screened = (pa[:, cs] * d / (d * d + 0.25)).astype(BF16)
            ubuf[slot, pl.ds(w * NST, NST), cs] = jnp.dot(
                lbuf[slot], screened, preferred_element_type=F32
            ).astype(BF16)

    def first_loop(count, slot_of, loads=False):
        def step(i, carry):
            c = i % NCHUNK
            if loads:
                @pl.when(i < NCHUNK)
                def _():
                    for copy in pole_copies(c):
                        copy.wait()
            first(slot_of(i // NCHUNK), c)
            return carry

        lax.fori_loop(0, count * NCHUNK, step, 0)

    def second(rslot):
        xs, ys = (x + rslot // 2) % 4, (ylo + rslot) % 2
        uslot = ((xs - z + 4) % 4) * 2 + (ys + core) % 2
        term = lax.dot_general(
            ubuf[uslot], rbuf[rslot], (((1,), (1,)), ((), ())), preferred_element_type=F32
        )
        for h in range(2):
            sig[pl.ds(h * 2 * NST, 2 * NST), :] += term[:, h * LANES:(h + 1) * LANES]

    def second_loop(count, slot_of):
        def step(i, carry):
            second(slot_of(i))
            return carry

        lax.fori_loop(0, count, step, 0)

    sig[...] = jnp.zeros_like(sig)
    own_l.wait()
    l_c1.wait_recv()
    first_loop(2, lambda i: i, loads=True)

    l_zm.wait_recv()
    a1 = send(lbuf.at[6, lo], lbuf.at[4, lo], lsend.at[3], lrecv.at[3], device(dz=1))
    a2 = send(lbuf.at[6], lbuf.at[7], lsend.at[4], lrecv.at[4], device(dc=1))
    l_zp.wait_recv()
    a3 = send(lbuf.at[2, hi], lbuf.at[4, hi], lsend.at[5], lrecv.at[5], device(dz=3))
    a4 = send(lbuf.at[2], lbuf.at[3], lsend.at[6], lrecv.at[6], device(dc=1))
    r_xm.wait_recv()
    b1 = send(rbuf.at[6, lo], rbuf.at[4, lo], rsend.at[3], rrecv.at[3], device(dx=1))
    r_xp.wait_recv()
    b2 = send(rbuf.at[2, hi], rbuf.at[4, hi], rsend.at[4], rrecv.at[4], device(dx=3))
    r_y1.wait_recv()
    b3 = send(rbuf.at[1], rbuf.at[7], rsend.at[5], rrecv.at[5], device(dx=1))
    b4 = send(rbuf.at[1], rbuf.at[3], rsend.at[6], rrecv.at[6], device(dx=3))

    first_loop(2, lambda i: 6 - 4 * i)
    a1.wait_recv()
    a3.wait_recv()
    a5 = send(lbuf.at[4], lbuf.at[5], lsend.at[7], lrecv.at[7], device(dc=1))
    b1.wait_recv()
    b2.wait_recv()
    b5 = send(rbuf.at[4], rbuf.at[5], rsend.at[7], rrecv.at[7], device(flip=1))
    a2.wait_recv()
    a4.wait_recv()
    first_loop(2, lambda i: 7 - 4 * i)
    a5.wait_recv()
    first_loop(2, lambda i: 4 + i)

    own_r.wait()
    second_loop(2, lambda i: i)
    second_loop(3, lambda i: 2 + 2 * i)
    b3.wait_recv()
    b4.wait_recv()
    b5.wait_recv()
    second_loop(3, lambda i: 3 + 2 * i)

    def build(t, carry):
        dc, dx, dy, dz = t // 64, (t // 16) % 4, (t // 4) % 4, t % 4
        xx, yy, zz, cc = (x + dx) % 4, (y + dy) % 4, (z + dz) % 4, (core + dc) % 2
        owner = ((((xx * 2 + yy % 2) * 4 + zz) * 2 + cc) * 2) + yy // 2
        for r in range(2):
            tiles[t, pl.ds(4 * r, 4), :] = sig[pl.ds(owner * 2 + r, 4, stride=NST), :]
        return carry

    lax.fori_loop(64, 128, build, 0)
    s = send(tiles.at[pl.ds(64, 64)], in_a, ssend.at[0], srecv.at[0], device(dc=1))
    lax.fori_loop(0, 64, build, 0)
    s.wait_recv()
    vx[...] = tiles[pl.ds(0, 64)] + in_a[...]

    def stage(value, landing, at, shift):
        n = landing.shape[1]
        copies = [
            send(value.at[pl.ds(k * n, n)], landing.at[k - 1], ssend.at[at + k], srecv.at[at + k], shift(k))
            for k in (2, 1, 3)
        ]
        total = value[pl.ds(0, n)]
        for copy in copies:
            copy.wait_recv()
        for k in range(3):
            total = total + landing[k]
        return total

    vy[...] = stage(vx, in_x, 0, lambda k: device(dx=k))
    vz[...] = stage(vy, in_y, 3, lambda k: device(dy=k))
    out[...] = stage(vz, in_z, 6, lambda k: device(dz=k))[0]
    for copy in started:
        copy.wait_send()


def body(freq_index, band_energy, pole_amp, pole_freq, left_pieces, right_pieces):
    smem = pl.BlockSpec(memory_space=pltpu.SMEM)
    anywhere = pl.BlockSpec(memory_space=pl.ANY)
    tile = (8, LANES)
    dma = pltpu.SemaphoreType.DMA
    result = pl.pallas_call(
        kernel,
        out_shape=jax.ShapeDtypeStruct(tile, F32),
        in_specs=[smem, smem, anywhere, anywhere, anywhere, anywhere],
        out_specs=pl.BlockSpec(memory_space=pltpu.VMEM),
        scratch_shapes=[
            pltpu.VMEM((TILE, TILE), F32),
            pltpu.VMEM((TILE, TILE), F32),
            pltpu.VMEM((8, NST, TILE), BF16),
            pltpu.VMEM((8, NST, TILE), BF16),
            pltpu.VMEM((8, 2 * NST, TILE), BF16),
            pltpu.VMEM((4 * NST, LANES), F32),
            pltpu.VMEM((128,) + tile, F32),
            pltpu.VMEM((64,) + tile, F32),
            pltpu.VMEM((64,) + tile, F32),
            pltpu.VMEM((3, 16) + tile, F32),
            pltpu.VMEM((16,) + tile, F32),
            pltpu.VMEM((3, 4) + tile, F32),
            pltpu.VMEM((4,) + tile, F32),
            pltpu.VMEM((3, 1) + tile, F32),
            dma((2 * NCHUNK,)), dma((2,)),
            dma((8,)), dma((8,)), dma((8,)), dma((8,)), dma((10,)), dma((10,)),
        ],
        compiler_params=pltpu.CompilerParams(
            collective_id=0, has_side_effects=True, vmem_limit_bytes=56 << 20
        ),
        name="self_energy",
    )(freq_index, band_energy, pole_freq, pole_amp, left_pieces, right_pieces)
    return result.reshape(2, 2, 2, LANES).transpose(2, 0, 1, 3).reshape(2, 2, 2 * LANES)


def solution(mesh):
    in_specs = (
        P(),
        P(),
        P("row", "col"),
        P("row", "col"),
        P(("col", "band"), None, "row"),
        P(("row", "band"), None, "col"),
    )
    out_specs = P(None, ("row", "col", "band"), None)
    return jax.shard_map(body, mesh=mesh, in_specs=in_specs, out_specs=out_specs, check_vma=False)
```

time: 393 us -> 62.7 us (0.16)
  the two profiles are of different devices: /device:TPU:1 before, /device:TPU:0 now
where the time goes in v1:
time: 62.7 us; the launch traced here: 62.5 us
  Pallas kernels  61.2 us (98%)
  local copies, waits for them, and re-layouts  1.29 us (2%)
    pallas_call x1, Pallas kernels, body(): pl.pallas_call(kernel, out_shape=jax.ShapeDtypeStruct(tile, F32), in_spec...  61.2 us

profile of v1, /device:TPU:0, one launch (start us, length us, event | category | flops | bytes accessed | tf_op | source)
XLA Modules:
  0.0 62.5 jit_solution(1606322191945902509)
XLA Ops:
  0.0 61.2 %self_energy.1 = f32[8,128]{1,0:T(8,128)} custom-call(s32[2]{0:T(128)} %freq_index.1, f32[16]{0:T(128)} %band_energy.1, f32[1024,1024]{1,0:T(8,128)} %pole_freq.1, f32[1024,1024]{1,0:T(8,128)} %pole_amp.1, bf16[1,256,1024]{2,1,0:T(8,128)(2,1)} %left.1, bf16[1,256,1024]{2,1,0:T(8,128)(2,1)} %right.1), custom_call_target="tpu_custom_call" | custom-call | tf_op jit(solution)/shard_map/self_energy/pallas_call | solution.py:201
  61.2 0.7 %copy.7 = f32[2,2,2,128]{3,2,1,0:T(2,128)S(1)} copy(f32[2,2,2,128]{3,0,2,1:T(2,128)} %bitcast.3) | data formatting | bytes 8192 | tf_op jit(solution)/shard_map/transpose | solution.py:229
  61.9 0.6 reshape.7

commit v2 on v1

v2 whole, which is shorter than its diff:
```python
import jax
import jax.numpy as jnp
from jax import lax
from jax.experimental import pallas as pl
from jax.experimental.pallas import tpu as pltpu
from jax.sharding import PartitionSpec as P

MESH = pl.DeviceIdType.MESH
F32 = jnp.float32
BF16 = jnp.bfloat16

NST = 256
TILE = 1024
HALF = NST // 2
CHUNK = 512
NCHUNK = TILE // CHUNK
SHARE = 32
LANES = 128


def kernel(freq_hbm, energy_hbm, pole_freq, pole_amp, left, right, out,
           freq_index, band_energy, pf, pa, lbuf, rbuf, ubuf, sig, tiles, in_a, total, in_f,
           load_sem, own_sem, lsend, lrecv, rsend, rrecv, ssend, srecv, plane_sem, all_sem):
    row, col, yhi = lax.axis_index("row"), lax.axis_index("col"), lax.axis_index("band")
    x, ylo, z, core = row // 2, row % 2, col // 2, col % 2
    y = yhi * 2 + ylo

    def device(dx=0, dy=0, dz=0, dc=0, flip=0):
        yy = (y + dy) % 4
        return {
            "row": ((x + dx) % 4) * 2 + (yy % 2 + flip) % 2,
            "col": ((z + dz) % 4) * 2 + (core + dc) % 2,
            "band": yy // 2,
        }

    def pole_copies(c):
        cs = pl.ds(pl.multiple_of(c * CHUNK, CHUNK), CHUNK)
        return (
            pltpu.make_async_copy(pole_freq.at[:, cs], pf.at[:, cs], load_sem.at[c]),
            pltpu.make_async_copy(pole_amp.at[:, cs], pa.at[:, cs], load_sem.at[NCHUNK + c]),
        )

    own_l = pltpu.make_async_copy(left.at[0], lbuf.at[0], own_sem.at[0])
    own_r = pltpu.make_async_copy(right.at[0], rbuf.at[0], own_sem.at[1])
    scalar_loads = (
        pltpu.make_async_copy(freq_hbm, freq_index, own_sem.at[2]),
        pltpu.make_async_copy(energy_hbm, band_energy, own_sem.at[3]),
    )
    for copy in (own_l,) + scalar_loads:
        copy.start()
    for copy in pole_copies(0):
        copy.start()

    barrier = pltpu.get_barrier_semaphore()
    peers = [device(dc=1)]
    for k in (1, 2, 3):
        peers += [device(dx=k), device(dy=k), device(dz=k)]
    for peer in peers:
        pl.semaphore_signal(barrier, inc=1, device_id=peer, device_id_type=MESH)
    pl.semaphore_wait(barrier, len(peers))

    started = []

    def send(src, dst, send_sem, recv_sem, to):
        copy = pltpu.make_async_remote_copy(
            src_ref=src, dst_ref=dst, send_sem=send_sem, recv_sem=recv_sem,
            device_id=to, device_id_type=MESH,
        )
        copy.start()
        started.append(copy)
        return copy

    lo, hi = pl.ds(0, HALF), pl.ds(HALF, HALF)
    quarter = [pl.ds(k * (HALF // 2), HALF // 2) for k in range(4)]
    via_y, via_x = pl.ds(HALF, SHARE), pl.ds(HALF + SHARE, HALF - SHARE)
    l_at, r_at = iter(range(7)), iter(range(18))

    def send_l(src, slot, to):
        k = next(l_at)
        return send(src, lbuf.at[slot], lsend.at[k], lrecv.at[k], to)

    def send_r(source, slot, part, to):
        k = next(r_at)
        ref = right.at[0, part] if source is None else rbuf.at[source, part]
        return send(ref, rbuf.at[slot, part], rsend.at[k], rrecv.at[k], to)

    near, far = 6 - 4 * core, 2 + 4 * core
    ahead, behind = device(dz=1 + 2 * core), device(dz=3 - 2 * core)
    other, across, xup, xdown = device(dc=1), device(flip=1), device(dx=1), device(dx=3)
    l_near = send_l(left.at[0], near, ahead)
    l_c1 = send_l(left.at[0], 1, other)
    r_up = [send_r(None, 6, part, xup) for part in (lo, quarter[2])]
    r_down = [send_r(None, 2, part, xdown) for part in (hi, quarter[0])]
    r_across = [send_r(None, 1, part, across) for part in (lo, hi)]
    for k in (1, 2, 3):
        pl.semaphore_signal(plane_sem, inc=1, device_id=device(dy=k), device_id_type=MESH)
    own_r.start()
    for c in range(1, NCHUNK):
        for copy in pole_copies(c):
            copy.start()

    def scalars(slot):
        zs, cs = (z + slot // 2) % 4, (core + slot) % 2
        energy = band_energy[(zs * 2 + cs) * 2 + yhi]
        return [-4.0 + 0.25 * freq_index[w].astype(F32) - energy for w in range(2)]

    def first(slot, c):
        cs = pl.ds(pl.multiple_of(c * CHUNK, CHUNK), CHUNK)
        shifts = scalars(slot)
        for w in range(2):
            d = shifts[w] - pf[:, cs]
            screened = (pa[:, cs] * d / (d * d + 0.25)).astype(BF16)
            ubuf[slot, pl.ds(w * NST, NST), cs] = jnp.dot(
                lbuf[slot], screened, preferred_element_type=F32
            ).astype(BF16)

    def first_loop(count, slot_of, loads=False):
        def step(i, carry):
            c = i % NCHUNK
            if loads:
                @pl.when(i < NCHUNK)
                def _():
                    for copy in pole_copies(c):
                        copy.wait()
            first(slot_of(i // NCHUNK), c)
            return carry

        lax.fori_loop(0, count * NCHUNK, step, 0)

    def second(rslot):
        xs, ys = (x + rslot // 2) % 4, (ylo + rslot) % 2
        uslot = ((xs - z + 4) % 4) * 2 + (ys + core) % 2
        term = lax.dot_general(
            ubuf[uslot], rbuf[rslot], (((1,), (1,)), ((), ())), preferred_element_type=F32
        )
        for h in range(2):
            sig[pl.ds(h * 2 * NST, 2 * NST), :] += term[:, h * LANES:(h + 1) * LANES]

    def second_loop(count, slot_of):
        def step(i, carry):
            second(slot_of(i))
            return carry

        lax.fori_loop(0, count, step, 0)

    sig[...] = jnp.zeros_like(sig)
    for copy in (own_l,) + scalar_loads:
        copy.wait()
    first_loop(1, lambda i: 0, loads=True)
    l_near.wait_send()
    started.remove(l_near)
    l_far = send_l(left.at[0], far, behind)
    l_c1.wait_recv()
    first_loop(1, lambda i: 1)

    pl.semaphore_wait(plane_sem, 3)
    for k in (1, 2, 3):
        pl.semaphore_signal(all_sem, inc=1, device_id=device(dz=k), device_id_type=MESH)
    l_near.wait_recv()
    l_c2 = send_l(lbuf.at[near], near + 1, other)
    l_a = send_l(lbuf.at[near], 4, ahead)
    r_up[0].wait_recv()
    r_a = send_r(6, 4, lo, xup)
    r_up.append(send_r(None, 6, quarter[3], xup))
    r_down[0].wait_recv()
    r_b = send_r(2, 4, hi, xdown)
    r_down.append(send_r(None, 2, quarter[1], xdown))
    r_across[0].wait_recv()
    r_up_q = [send_r(1, 7, lo, xup)]
    r_down_q = [send_r(1, 3, lo, xdown)]
    first_loop(1, lambda i: near)
    l_c2.wait_recv()
    first_loop(1, lambda i: far + 1)

    r_across[1].wait_recv()
    r_up_q.append(send_r(1, 7, via_x, xup))
    r_down_q.append(send_r(1, 3, via_x, xdown))
    r_up[1].wait_recv()
    r_c = [send_r(6, 7, via_y, across), send_r(2, 3, via_y, across)]
    l_far.wait_recv()
    l_c3 = send_l(lbuf.at[far], far + 1, other)
    first_loop(1, lambda i: far)
    r_a.wait_recv()
    r_c.append(send_r(4, 5, lo, across))
    r_b.wait_recv()
    r_c.append(send_r(4, 5, hi, across))
    l_c3.wait_recv()
    first_loop(1, lambda i: near + 1)
    l_a.wait_recv()
    l_c4 = send_l(lbuf.at[4], 5, other)
    first_loop(1, lambda i: 4)
    l_c4.wait_recv()
    first_loop(1, lambda i: 5)

    own_r.wait()
    second_loop(2, lambda i: i)
    for copy in r_up[2:] + r_down[1:]:
        copy.wait_recv()
    second_loop(3, lambda i: 2 + 2 * i)
    for copy in r_up_q + r_down_q + r_c[:2]:
        copy.wait_recv()
    second_loop(2, lambda i: 3 + 4 * i)
    for copy in r_c[2:]:
        copy.wait_recv()
    second(5)

    def build(q, carry):
        base = (q // 8) * 128 + (q % 8) * 8
        for cc in range(2):
            for hh in range(2):
                at = pl.multiple_of(base + cc * 512 + hh * 64, 8)
                for r in range(2):
                    rows = pl.ds(q * 8 + cc * 4 + hh * 2 + r, 4, stride=NST)
                    tiles[pl.ds(at + 4 * r, 4), :] = sig[rows, :]
        return carry

    lax.fori_loop(0, 32, build, 0)

    def part(k, n):
        return pl.ds(pl.multiple_of(k * n, n), n)

    s = send(tiles.at[part(1 - core, 512)], in_a, ssend.at[0], srecv.at[0], other)
    pl.semaphore_wait(all_sem, 3)
    s.wait_recv()
    total[...] = tiles[part(core, 512), :] + in_a[...]

    def term(k):
        dx, dy, dz = k // 16, (k // 4) % 4, k % 4
        to = (((x + dx) % 4) * 4 + (y + dy) % 4) * 4 + (z + dz) % 4
        copy = pltpu.make_async_remote_copy(
            src_ref=total.at[part(to, 8)], dst_ref=in_f.at[part(k - 1, 8)], send_sem=ssend.at[1], recv_sem=srecv.at[1],
            device_id=device(dx=dx, dy=dy, dz=dz), device_id_type=MESH,
        )
        copy.start()

    for k in range(1, 64):
        term(k)
    every = pltpu.make_async_remote_copy(
        src_ref=total.at[pl.ds(0, 504)], dst_ref=in_f, send_sem=ssend.at[1], recv_sem=srecv.at[1],
        device_id=other, device_id_type=MESH,
    )
    me = part((x * 4 + y) * 4 + z, 8)
    every.wait_recv()
    tile = total[me, :] + jnp.sum(in_f[...].reshape(63, 8, LANES), axis=0)
    started.append(every)
    for r in range(2):
        for h in range(2):
            for w in range(2):
                at = 4 * r + 2 * h + w
                out[w, pl.ds(r, 1), pl.ds(h * LANES, LANES)] = tile[at:at + 1, :]
    for copy in started:
        copy.wait_send()


def body(freq_index, band_energy, pole_amp, pole_freq, left_pieces, right_pieces):
    anywhere = pl.BlockSpec(memory_space=pl.ANY)
    dma = pltpu.SemaphoreType.DMA
    return pl.pallas_call(
        kernel,
        out_shape=jax.ShapeDtypeStruct((2, 2, 2 * LANES), F32),
        in_specs=[anywhere] * 6,
        out_specs=pl.BlockSpec(memory_space=pltpu.VMEM),
        scratch_shapes=[
            pltpu.SMEM((2,), jnp.int32),
            pltpu.SMEM((16,), F32),
            pltpu.VMEM((TILE, TILE), F32),
            pltpu.VMEM((TILE, TILE), F32),
            pltpu.VMEM((8, NST, TILE), BF16),
            pltpu.VMEM((8, NST, TILE), BF16),
            pltpu.VMEM((8, 2 * NST, TILE), BF16),
            pltpu.VMEM((4 * NST, LANES), F32),
            pltpu.VMEM((1024, LANES), F32),
            pltpu.VMEM((512, LANES), F32),
            pltpu.VMEM((512, LANES), F32),
            pltpu.VMEM((504, LANES), F32),
            dma((2 * NCHUNK,)), dma((4,)),
            dma((7,)), dma((7,)), dma((18,)), dma((18,)), dma((2,)), dma((2,)),
            pltpu.SemaphoreType.REGULAR, pltpu.SemaphoreType.REGULAR,
        ],
        compiler_params=pltpu.CompilerParams(
            collective_id=0, has_side_effects=True, vmem_limit_bytes=56 << 20
        ),
        name="self_energy",
    )(freq_index, band_energy, pole_freq, pole_amp, left_pieces, right_pieces)


def solution(mesh):
    in_specs = (
        P(),
        P(),
        P("row", "col"),
        P("row", "col"),
        P(("col", "band"), None, "row"),
        P(("row", "band"), None, "col"),
    )
    out_specs = P(None, ("row", "col", "band"), None)
    return jax.shard_map(body, mesh=mesh, in_specs=in_specs, out_specs=out_specs, check_vma=False)
```

time: 62.7 us -> 54.8 us (0.87)
  the two profiles are of different devices: /device:TPU:0 before, /device:TPU:1 now
where the time goes in v2:
time: 54.8 us; the launch traced here: 54.7 us
  Pallas kernels  53.4 us (97%)
  local copies, waits for them, and re-layouts  1.28 us (2%)
    pallas_call x1, Pallas kernels, body(): pl.pallas_call(kernel, out_shape=jax.ShapeDtypeStruct((2, 2, 2 * LANES),...  53.4 us
    unnamed x1, local copies, waits for them, and re-layouts  1.28 us

profile of v2, /device:TPU:1, one launch (start us, length us, event | category | flops | bytes accessed | tf_op | source)
XLA Modules:
  0.0 54.7 jit_solution(3232343436031297253)
XLA Ops:
  0.0 53.4 %self_energy.1 = f32[2,2,256]{2,1,0:T(2,128)} custom-call(s32[2]{0:T(128)} %freq_hbm.1, f32[16]{0:T(128)} %energy_hbm.1, f32[1024,1024]{1,0:T(8,128)} %pole_freq.1, f32[1024,1024]{1,0:T(8,128)} %pole_amp.1, bf16[1,256,1024]{2,1,0:T(8,128)(2,1)} %left.1, bf16[1,256,1024]{2,1,0:T(8,128)(2,1)} %right.1), custom_call_target="tpu_custom_call" | custom-call | tf_op jit(solution)/shard_map/self_energy/pallas_call | solution.py:258
  53.4 1.3 %copy.8 = f32[2,2,256]{2,1,0:T(2,128)} copy(f32[2,2,256]{2,1,0:T(2,128)} %self_energy.1) | data formatting | bytes 8192

commit v3 on v2

v3 whole, which is shorter than its diff:
```python
import jax
import jax.numpy as jnp
from jax import lax
from jax.experimental import pallas as pl
from jax.experimental.pallas import tpu as pltpu
from jax.sharding import PartitionSpec as P

MESH = pl.DeviceIdType.MESH
F32 = jnp.float32
BF16 = jnp.bfloat16

NST = 256
TILE = 1024
HALF = NST // 2
LANES = 128


def kernel(freq_hbm, energy_hbm, pole_freq, pole_amp, left, right, out,
           freq_index, band_energy, pf, pa, sbuf_0, sbuf_1, lbuf, rbuf, ubuf, sig, tiles, in_a, total, in_f,
           load_sem, own_sem, lsend, lrecv, rsend, rrecv, ssend, srecv, plane_sem, all_sem):
    row, col, yhi = lax.axis_index("row"), lax.axis_index("col"), lax.axis_index("band")
    x, ylo, z, core = row // 2, row % 2, col // 2, col % 2
    y = yhi * 2 + ylo

    def device(dx=0, dy=0, dz=0, dc=0, flip=0):
        yy = (y + dy) % 4
        return {
            "row": ((x + dx) % 4) * 2 + (yy % 2 + flip) % 2,
            "col": ((z + dz) % 4) * 2 + (core + dc) % 2,
            "band": yy // 2,
        }

    own_l = pltpu.make_async_copy(left.at[0], lbuf.at[0], own_sem.at[0])
    own_r = pltpu.make_async_copy(right.at[0], rbuf.at[0], own_sem.at[1])
    scalar_loads = (
        pltpu.make_async_copy(freq_hbm, freq_index, own_sem.at[2]),
        pltpu.make_async_copy(energy_hbm, band_energy, own_sem.at[3]),
    )
    pole_loads = (
        pltpu.make_async_copy(pole_freq, pf, load_sem.at[0]),
        pltpu.make_async_copy(pole_amp, pa, load_sem.at[1]),
    )
    for copy in scalar_loads + pole_loads + (own_l, own_r):
        copy.start()

    barrier = pltpu.get_barrier_semaphore()
    peers = [device(dc=1)]
    for k in (1, 2, 3):
        peers += [device(dx=k), device(dy=k), device(dz=k)]
    for peer in peers:
        pl.semaphore_signal(barrier, inc=1, device_id=peer, device_id_type=MESH)
    pl.semaphore_wait(barrier, len(peers))

    started = []

    def plan(src, dst, send_sem, recv_sem, to):
        copy = pltpu.make_async_remote_copy(
            src_ref=src, dst_ref=dst, send_sem=send_sem, recv_sem=recv_sem,
            device_id=to, device_id_type=MESH,
        )
        started.append(copy)
        return copy

    def start(*copies):
        for copy in copies:
            copy.start()

    def arrive(*copies):
        for copy in copies:
            copy.wait_recv()

    l_at, r_at = iter(range(7)), iter(range(20))

    def plan_l(src, slot, to):
        k = next(l_at)
        return plan(src, lbuf.at[slot], lsend.at[k], lrecv.at[k], to)

    def plan_r(source, slot, begin, end, to):
        k, part = next(r_at), pl.ds(begin, end - begin)
        ref = right.at[0, part] if source is None else rbuf.at[source, part]
        return plan(ref, rbuf.at[slot, part], rsend.at[k], rrecv.at[k], to)

    near, far = 6 - 4 * core, 2 + 4 * core
    near1, far1 = near + 1, far + 1
    ahead, behind = device(dz=1 + 2 * core), device(dz=3 - 2 * core)
    other, across, xup, xdown = device(dc=1), device(flip=1), device(dx=1), device(dx=3)
    z_line = [device(dz=k) for k in (1, 2, 3)]

    l_near = plan_l(left.at[0], near, ahead)
    l_own1 = plan_l(left.at[0], 1, other)
    l_far = plan_l(left.at[0], far, behind)
    l_next = plan_l(lbuf.at[near], 4, ahead)
    l_near1 = plan_l(lbuf.at[near], near1, other)
    l_far1 = plan_l(lbuf.at[far], far1, other)
    l_five = plan_l(lbuf.at[4], 5, other)

    up = [plan_r(None, 6, begin, end, xup) for begin, end in ((0, 128), (128, 192), (192, 256))]
    down = [plan_r(None, 2, begin, end, xdown) for begin, end in ((128, 256), (0, 64), (64, 128))]
    over = [plan_r(None, 1, begin, end, across) for begin, end in ((0, 128), (128, 256))]
    up_on, down_on = plan_r(6, 4, 0, 128, xup), plan_r(2, 4, 128, 256, xdown)
    over_up = [plan_r(6, 7, begin, end, across) for begin, end in ((0, 64), (64, 96))]
    over_down = [plan_r(2, 3, begin, end, across) for begin, end in ((192, 256), (160, 192))]
    up_q, down_q = plan_r(1, 7, 96, 256, xup), plan_r(1, 3, 0, 160, xdown)
    over_on = [plan_r(4, 5, begin, end, across) for begin, end in ((64, 128), (128, 192))]
    up_far, down_far = plan_r(7, 5, 0, 64, xup), plan_r(3, 5, 192, 256, xdown)

    start(l_near, l_own1, up[0], down[0], over[0], up[1], down[1], over[1])
    for k in (1, 2, 3):
        pl.semaphore_signal(plane_sem, inc=1, device_id=device(dy=k), device_id_type=MESH)
    def scalars(slot):
        zs, cs = (z + slot // 2) % 4, (core + slot) % 2
        energy = band_energy[(zs * 2 + cs) * 2 + yhi]
        return [-4.0 + 0.25 * freq_index[w].astype(F32) - energy for w in range(2)]

    sbufs = (sbuf_0, sbuf_1)

    def screen(slot, at):
        shifts = scalars(slot)
        for w in range(2):
            d = shifts[w] - pf[...]
            sbufs[at][w] = (pa[...] * d / (d * d + 0.25)).astype(BF16)

    def first(slot, at):
        for w in range(2):
            ubuf[slot, pl.ds(w * NST, NST), :] = jnp.dot(
                lbuf[slot], sbufs[at][w], preferred_element_type=F32
            ).astype(BF16)

    def second(rslot):
        xs, ys = (x + rslot // 2) % 4, (ylo + rslot) % 2
        uslot = ((xs - z + 4) % 4) * 2 + (ys + core) % 2
        term = lax.dot_general(
            ubuf[uslot], rbuf[rslot], (((1,), (1,)), ((), ())), preferred_element_type=F32
        )
        for h in range(2):
            sig[pl.ds(h * 2 * NST, 2 * NST), :] += term[:, h * LANES:(h + 1) * LANES]

    sig[...] = jnp.zeros_like(sig)

    def at_own():
        own_l.wait()

    def at_partner():
        l_near.wait_send()
        start(l_far)
        arrive(l_own1)

    def at_near():
        arrive(up[0])
        start(up_on, up[2])
        arrive(down[0])
        start(down_on, down[2], over_up[0], over_down[0], over_up[1], over_down[1])
        arrive(l_near)
        start(l_next, l_near1)
        pl.semaphore_wait(plane_sem, 3)
        for to in z_line:
            pl.semaphore_signal(all_sem, inc=1, device_id=to, device_id_type=MESH)

    def at_far1():
        arrive(l_near1)

    def at_far():
        arrive(*over)
        start(up_q, down_q)
        arrive(l_far)
        start(l_far1)

    def at_near1():
        arrive(l_far1)
        arrive(up_on)
        start(over_on[0])
        arrive(down_on)
        start(over_on[1])
        arrive(over_up[0])
        start(up_far)

    def at_4():
        arrive(l_next)
        start(l_five)
        arrive(over_down[0])
        start(down_far)

    def at_5():
        arrive(l_five)

    heads = (at_own, at_partner, at_near, at_far1, at_far, at_near1, at_4, at_5)

    def slot_of(k):
        m = k - 2
        middle = near + ((m + m // 2) % 2) * (far - near) + m % 2
        return jnp.where(k < 2, k, jnp.where(k < 6, middle, m))

    def band_pair(pair, carry):
        for j in range(2):
            screen(slot_of(2 * pair + j), j)
        for j in range(2):
            k = 2 * pair + j
            for n in range(j, 8, 2):
                pl.when(k == n)(heads[n])
            first(slot_of(k), j)
        return carry

    for copy in scalar_loads + pole_loads:
        copy.wait()
    lax.fori_loop(0, 4, band_pair, 0)

    def at_second_0():
        own_r.wait()

    def at_second_2():
        arrive(*up[1:], *down[1:])

    def at_second_5():
        arrive(up_q, down_q, over_up[1], over_down[1])

    def at_second_7():
        arrive(*over_on, up_far, down_far)

    def second_step(i, carry):
        for n, head in ((0, at_second_0), (2, at_second_2), (5, at_second_5), (7, at_second_7)):
            pl.when(i == n)(head)
        t = i - 5
        second(jnp.where(i < 2, i, jnp.where(i < 5, 2 * (i - 1), 3 + 4 * t - 6 * (t // 2))))
        return carry

    lax.fori_loop(0, 8, second_step, 0)

    def build(q, carry):
        base = (q // 8) * 128 + (q % 8) * 8
        for cc in range(2):
            for hh in range(2):
                at = pl.multiple_of(base + cc * 512 + hh * 64, 8)
                for r in range(2):
                    rows = pl.ds(q * 8 + cc * 4 + hh * 2 + r, 4, stride=NST)
                    tiles[pl.ds(at + 4 * r, 4), :] = sig[rows, :]
        return carry

    lax.fori_loop(0, 32, build, 0)

    def part(k, n):
        return pl.ds(pl.multiple_of(k * n, n), n)

    s = plan(tiles.at[part(1 - core, 512)], in_a, ssend.at[0], srecv.at[0], other)
    s.start()
    pl.semaphore_wait(all_sem, 3)
    s.wait_recv()
    total[...] = tiles[part(core, 512), :] + in_a[...]

    def term(k):
        dx, dy, dz = k // 16, (k // 4) % 4, k % 4
        to = (((x + dx) % 4) * 4 + (y + dy) % 4) * 4 + (z + dz) % 4
        copy = pltpu.make_async_remote_copy(
            src_ref=total.at[part(to, 8)], dst_ref=in_f.at[part(k - 1, 8)], send_sem=ssend.at[1], recv_sem=srecv.at[1],
            device_id=device(dx=dx, dy=dy, dz=dz), device_id_type=MESH,
        )
        copy.start()

    for k in range(1, 64):
        term(k)
    every = pltpu.make_async_remote_copy(
        src_ref=total.at[pl.ds(0, 504)], dst_ref=in_f, send_sem=ssend.at[1], recv_sem=srecv.at[1],
        device_id=other, device_id_type=MESH,
    )
    me = part((x * 4 + y) * 4 + z, 8)
    every.wait_recv()
    tile = total[me, :] + jnp.sum(in_f[...].reshape(63, 8, LANES), axis=0)
    started.append(every)
    for r in range(2):
        for h in range(2):
            for w in range(2):
                at = 4 * r + 2 * h + w
                out[w, pl.ds(r, 1), pl.ds(h * LANES, LANES)] = tile[at:at + 1, :]
    for copy in started:
        if copy is not l_near:
            copy.wait_send()


def body(freq_index, band_energy, pole_amp, pole_freq, left_pieces, right_pieces):
    anywhere = pl.BlockSpec(memory_space=pl.ANY)
    dma = pltpu.SemaphoreType.DMA
    return pl.pallas_call(
        kernel,
        out_shape=jax.ShapeDtypeStruct((2, 2, 2 * LANES), F32),
        in_specs=[anywhere] * 6,
        out_specs=pl.BlockSpec(memory_space=pltpu.VMEM),
        scratch_shapes=[
            pltpu.SMEM((2,), jnp.int32),
            pltpu.SMEM((16,), F32),
            pltpu.VMEM((TILE, TILE), F32),
            pltpu.VMEM((TILE, TILE), F32),
            pltpu.VMEM((2, TILE, TILE), BF16),
            pltpu.VMEM((2, TILE, TILE), BF16),
            pltpu.VMEM((8, NST, TILE), BF16),
            pltpu.VMEM((8, NST, TILE), BF16),
            pltpu.VMEM((8, 2 * NST, TILE), BF16),
            pltpu.VMEM((4 * NST, LANES), F32),
            pltpu.VMEM((1024, LANES), F32),
            pltpu.VMEM((512, LANES), F32),
            pltpu.VMEM((512, LANES), F32),
            pltpu.VMEM((504, LANES), F32),
            dma((2,)), dma((4,)),
            dma((7,)), dma((7,)), dma((20,)), dma((20,)), dma((2,)), dma((2,)),
            pltpu.SemaphoreType.REGULAR, pltpu.SemaphoreType.REGULAR,
        ],
        compiler_params=pltpu.CompilerParams(
            collective_id=0, has_side_effects=True, vmem_limit_bytes=56 << 20
        ),
        name="self_energy",
    )(freq_index, band_energy, pole_freq, pole_amp, left_pieces, right_pieces)


def solution(mesh):
    in_specs = (
        P(),
        P(),
        P("row", "col"),
        P("row", "col"),
        P(("col", "band"), None, "row"),
        P(("row", "band"), None, "col"),
    )
    out_specs = P(None, ("row", "col", "band"), None)
    return jax.shard_map(body, mesh=mesh, in_specs=in_specs, out_specs=out_specs, check_vma=False)
```

time: 54.8 us -> 52.3 us (0.954)
  Pallas kernels: 53.4 us -> 50.9 us
    pallas_call x1, Pallas kernels: 53.4 us -> 50.9 us  [body(): pl.pallas_call(kernel, out_shape=jax.ShapeDtypeStruct((2, 2, 2 * LANES),...]
where the time goes in v3:
time: 52.3 us; the launch traced here: 52.1 us
  Pallas kernels  50.9 us (97%)
  local copies, waits for them, and re-layouts  1.28 us (2%)
    pallas_call x1, Pallas kernels, body(): pl.pallas_call(kernel, out_shape=jax.ShapeDtypeStruct((2, 2, 2 * LANES),...  50.9 us
    unnamed x1, local copies, waits for them, and re-layouts  1.28 us

profile of v3, /device:TPU:1, one launch (start us, length us, event | category | flops | bytes accessed | tf_op | source)
XLA Modules:
  0.0 52.1 jit_solution(871793034932816231)
XLA Ops:
  0.0 50.9 %self_energy.1 = f32[2,2,256]{2,1,0:T(2,128)} custom-call(s32[2]{0:T(128)} %freq_hbm.1, f32[16]{0:T(128)} %energy_hbm.1, f32[1024,1024]{1,0:T(8,128)} %pole_freq.1, f32[1024,1024]{1,0:T(8,128)} %pole_amp.1, bf16[1,256,1024]{2,1,0:T(8,128)(2,1)} %left.1, bf16[1,256,1024]{2,1,0:T(8,128)(2,1)} %right.1), custom_call_target="tpu_custom_call" | custom-call | tf_op jit(solution)/shard_map/self_energy/pallas_call | solution.py:281
  50.9 1.3 %copy.8 = f32[2,2,256]{2,1,0:T(2,128)} copy(f32[2,2,256]{2,1,0:T(2,128)} %self_energy.1) | data formatting | bytes 8192

commit v4 on v3

--- a/solution.py
+++ b/solution.py
@@ -126,9 +126,16 @@
                 lbuf[slot], sbufs[at][w], preferred_element_type=F32
             ).astype(BF16)
 
+    def order(i):
+        t = i - 5
+        return jnp.where(i < 2, i, jnp.where(i < 5, 2 * (i - 1), 3 + 4 * t - 6 * (t // 2)))
+
+    def uslot_of(rslot):
+        xs, ys = (x + rslot // 2) % 4, (ylo + rslot) % 2
+        return ((xs - z + 4) % 4) * 2 + (ys + core) % 2
+
     def second(rslot):
-        xs, ys = (x + rslot // 2) % 4, (ylo + rslot) % 2
-        uslot = ((xs - z + 4) % 4) * 2 + (ys + core) % 2
+        uslot = uslot_of(rslot)
         term = lax.dot_general(
             ubuf[uslot], rbuf[rslot], (((1,), (1,)), ((), ())), preferred_element_type=F32
         )
@@ -145,13 +152,16 @@
         start(l_far)
         arrive(l_own1)
 
-    def at_near():
+    def mid_near():
         arrive(up[0])
         start(up_on, up[2])
         arrive(down[0])
         start(down_on, down[2], over_up[0], over_down[0], over_up[1], over_down[1])
         arrive(l_near)
         start(l_next, l_near1)
+
+    def at_near():
+        mid_near()
         pl.semaphore_wait(plane_sem, 3)
         for to in z_line:
             pl.semaphore_signal(all_sem, inc=1, device_id=to, device_id_type=MESH)
@@ -159,9 +169,11 @@
     def at_far1():
         arrive(l_near1)
 
-    def at_far():
+    def mid_far():
         arrive(*over)
         start(up_q, down_q)
+
+    def at_far():
         arrive(l_far)
         start(l_far1)
 
@@ -174,9 +186,11 @@
         arrive(over_up[0])
         start(up_far)
 
-    def at_4():
+    def mid_4():
         arrive(l_next)
         start(l_five)
+
+    def at_4():
         arrive(over_down[0])
         start(down_far)
 
@@ -191,8 +205,10 @@
         return jnp.where(k < 2, k, jnp.where(k < 6, middle, m))
 
     def band_pair(pair, carry):
-        for j in range(2):
-            screen(slot_of(2 * pair + j), j)
+        screen(slot_of(2 * pair), 0)
+        for n, middle in ((2, mid_far), (3, mid_4)):
+            pl.when(pair == n)(middle)
+        screen(slot_of(2 * pair + 1), 1)
         for j in range(2):
             k = 2 * pair + j
             for n in range(j, 8, 2):
@@ -219,8 +235,7 @@
     def second_step(i, carry):
         for n, head in ((0, at_second_0), (2, at_second_2), (5, at_second_5), (7, at_second_7)):
             pl.when(i == n)(head)
-        t = i - 5
-        second(jnp.where(i < 2, i, jnp.where(i < 5, 2 * (i - 1), 3 + 4 * t - 6 * (t // 2))))
+        second(order(i))
         return carry
 
     lax.fori_loop(0, 8, second_step, 0)

time: 52.3 us -> 51.8 us (level)
  no operation moved by 1% of the time
where the time goes in v4:
time: 51.8 us; the launch traced here: 51.7 us
  Pallas kernels  50.4 us (97%)
  local copies, waits for them, and re-layouts  1.28 us (2%)
    pallas_call x1, Pallas kernels, body(): pl.pallas_call(kernel, out_shape=jax.ShapeDtypeStruct((2, 2, 2 * LANES),...  50.4 us
    unnamed x1, local copies, waits for them, and re-layouts  1.28 us

profile of v4, /device:TPU:1, one launch (start us, length us, event | category | flops | bytes accessed | tf_op | source)
XLA Modules:
  0.0 51.7 jit_solution(7944608152575720682)
XLA Ops:
  0.0 50.4 %self_energy.1 = f32[2,2,256]{2,1,0:T(2,128)} custom-call(s32[2]{0:T(128)} %freq_hbm.1, f32[16]{0:T(128)} %energy_hbm.1, f32[1024,1024]{1,0:T(8,128)} %pole_freq.1, f32[1024,1024]{1,0:T(8,128)} %pole_amp.1, bf16[1,256,1024]{2,1,0:T(8,128)(2,1)} %left.1, bf16[1,256,1024]{2,1,0:T(8,128)(2,1)} %right.1), custom_call_target="tpu_custom_call" | custom-call | tf_op jit(solution)/shard_map/self_energy/pallas_call | solution.py:296
  50.4 1.3 %copy.8 = f32[2,2,256]{2,1,0:T(2,128)} copy(f32[2,2,256]{2,1,0:T(2,128)} %self_energy.1) | data formatting | bytes 8192

commit v5 on v4

--- a/solution.py
+++ b/solution.py
@@ -259,13 +259,14 @@
     s.start()
     pl.semaphore_wait(all_sem, 3)
     s.wait_recv()
-    total[...] = tiles[part(core, 512), :] + in_a[...]
+    in_a[...] = tiles[part(core, 512), :] + in_a[...]
+    total[...] = in_a[...].reshape(64, 8, LANES).astype(BF16)
 
     def term(k):
         dx, dy, dz = k // 16, (k // 4) % 4, k % 4
         to = (((x + dx) % 4) * 4 + (y + dy) % 4) * 4 + (z + dz) % 4
         copy = pltpu.make_async_remote_copy(
-            src_ref=total.at[part(to, 8)], dst_ref=in_f.at[part(k - 1, 8)], send_sem=ssend.at[1], recv_sem=srecv.at[1],
+            src_ref=total.at[to], dst_ref=in_f.at[k - 1], send_sem=ssend.at[1], recv_sem=srecv.at[1],
             device_id=device(dx=dx, dy=dy, dz=dz), device_id_type=MESH,
         )
         copy.start()
@@ -273,12 +274,12 @@
     for k in range(1, 64):
         term(k)
     every = pltpu.make_async_remote_copy(
-        src_ref=total.at[pl.ds(0, 504)], dst_ref=in_f, send_sem=ssend.at[1], recv_sem=srecv.at[1],
+        src_ref=total.at[pl.ds(0, 63)], dst_ref=in_f, send_sem=ssend.at[1], recv_sem=srecv.at[1],
         device_id=other, device_id_type=MESH,
     )
     me = part((x * 4 + y) * 4 + z, 8)
     every.wait_recv()
-    tile = total[me, :] + jnp.sum(in_f[...].reshape(63, 8, LANES), axis=0)
+    tile = in_a[me, :] + jnp.sum(in_f[...].astype(F32), axis=0)
     started.append(every)
     for r in range(2):
         for h in range(2):
@@ -311,8 +312,8 @@
             pltpu.VMEM((4 * NST, LANES), F32),
             pltpu.VMEM((1024, LANES), F32),
             pltpu.VMEM((512, LANES), F32),
-            pltpu.VMEM((512, LANES), F32),
-            pltpu.VMEM((504, LANES), F32),
+            pltpu.VMEM((64, 8, LANES), BF16),
+            pltpu.VMEM((63, 8, LANES), BF16),
             dma((2,)), dma((4,)),
             dma((7,)), dma((7,)), dma((20,)), dma((20,)), dma((2,)), dma((2,)),
             pltpu.SemaphoreType.REGULAR, pltpu.SemaphoreType.REGULAR,

time: 51.8 us -> 50.6 us (0.977)
  Pallas kernels: 50.4 us -> 49.2 us
    pallas_call x1, Pallas kernels: 50.4 us -> 49.2 us  [body(): pl.pallas_call(kernel, out_shape=jax.ShapeDtypeStruct((2, 2, 2 * LANES),...]
where the time goes in v5:
time: 50.6 us; the launch traced here: 50.4 us
  Pallas kernels  49.2 us (97%)
  local copies, waits for them, and re-layouts  1.28 us (3%)
    pallas_call x1, Pallas kernels, body(): pl.pallas_call(kernel, out_shape=jax.ShapeDtypeStruct((2, 2, 2 * LANES),...  49.2 us
    unnamed x1, local copies, waits for them, and re-layouts  1.28 us

profile of v5, /device:TPU:1, one launch (start us, length us, event | category | flops | bytes accessed | tf_op | source)
XLA Modules:
  0.0 50.4 jit_solution(12273800448921458932)
XLA Ops:
  0.0 49.2 %self_energy.1 = f32[2,2,256]{2,1,0:T(2,128)} custom-call(s32[2]{0:T(128)} %freq_hbm.1, f32[16]{0:T(128)} %energy_hbm.1, f32[1024,1024]{1,0:T(8,128)} %pole_freq.1, f32[1024,1024]{1,0:T(8,128)} %pole_amp.1, bf16[1,256,1024]{2,1,0:T(8,128)(2,1)} %left.1, bf16[1,256,1024]{2,1,0:T(8,128)(2,1)} %right.1), custom_call_target="tpu_custom_call" | custom-call | tf_op jit(solution)/shard_map/self_energy/pallas_call | solution.py:297
  49.2 1.3 %copy.8 = f32[2,2,256]{2,1,0:T(2,128)} copy(f32[2,2,256]{2,1,0:T(2,128)} %self_energy.1) | data formatting | bytes 8192

commit v6 on v5

--- a/solution.py
+++ b/solution.py
@@ -271,7 +271,10 @@
         )
         copy.start()
 
-    for k in range(1, 64):
+    def hops(k):
+        return sum(min(d, 4 - d) for d in (k // 16, (k // 4) % 4, k % 4))
+
+    for k in sorted(range(1, 64), key=hops, reverse=True):
         term(k)
     every = pltpu.make_async_remote_copy(
         src_ref=total.at[pl.ds(0, 63)], dst_ref=in_f, send_sem=ssend.at[1], recv_sem=srecv.at[1],

time: 50.6 us -> 50.4 us (level)
  no operation moved by 1% of the time
where the time goes in v6:
time: 50.4 us; the launch traced here: 50.3 us
  Pallas kernels  49 us (97%)
  local copies, waits for them, and re-layouts  1.28 us (3%)
    pallas_call x1, Pallas kernels, body(): pl.pallas_call(kernel, out_shape=jax.ShapeDtypeStruct((2, 2, 2 * LANES),...  49 us
    unnamed x1, local copies, waits for them, and re-layouts  1.28 us

profile of v6, /device:TPU:1, one launch (start us, length us, event | category | flops | bytes accessed | tf_op | source)
XLA Modules:
  0.0 50.3 jit_solution(4350518535536928817)
XLA Ops:
  0.0 49.0 %self_energy.1 = f32[2,2,256]{2,1,0:T(2,128)} custom-call(s32[2]{0:T(128)} %freq_hbm.1, f32[16]{0:T(128)} %energy_hbm.1, f32[1024,1024]{1,0:T(8,128)} %pole_freq.1, f32[1024,1024]{1,0:T(8,128)} %pole_amp.1, bf16[1,256,1024]{2,1,0:T(8,128)(2,1)} %left.1, bf16[1,256,1024]{2,1,0:T(8,128)(2,1)} %right.1), custom_call_target="tpu_custom_call" | custom-call | tf_op jit(solution)/shard_map/self_energy/pallas_call | solution.py:300
  49.0 1.3 %copy.8 = f32[2,2,256]{2,1,0:T(2,128)} copy(f32[2,2,256]{2,1,0:T(2,128)} %self_energy.1) | data formatting | bytes 8192
